TPU v7x, 32 devices: a whole 2x2x4 slice. The times are simulated.
32 devices in a mesh: comp: 2 (over y), tile: 16 (over z, x, core).
Axes of the slice: x: 2, y: 2, z: 4, core: 2. Of those that a mesh axis runs over, the one named last changes fastest.
Arguments:
- model_state: float32 [2, 4, 12, 512, 1024], P('comp', None, None, 'tile'), may hold values from -6 to 6
- sea_mask: int32 [2, 512, 1024], P('comp', 'tile'), may hold values 0 or 1
- diffusion: float32 [2, 4], P('comp'), may hold values from 0.02 to 0.24
- vertical_mix: float32 [2, 4, 12, 12], P('comp'), may hold values from -0.4 to 0.4
- export_mix: float32 [2, 16, 4], P('comp'), may hold values from -3 to 3
- import_mix: float32 [2, 4, 16], P('comp'), may hold values from -1.5 to 1.5
- pair_source: int32 [2, 3072], P('comp', 'tile'), may hold values from 0 to 255
- pair_tile: int32 [2, 3072], P('comp', 'tile'), may hold values from 0 to 15, as said below
- pair_block: int32 [2, 3072], P('comp', 'tile'), may hold values from 0 to 255
- pair_count: int32 [2, 16], P('comp', 'tile'), may hold values from 144 to 192, as said below
- pair_weight: bfloat16 [2, 3072, 128, 128], P('comp', 'tile'), may hold values from -0.5 to 0.5
Outputs:
- advanced_state: float32 [2, 4, 12, 512, 1024], P('comp', None, None, 'tile')
Inputs may be any that keep to these rules, and one draw needn't show every extreme that they name: `pair_count`: slots at or beyond a tile's count are unused; in each component some tile uses all 192. `pair_tile`: among the used slots of one tile at most 24 name one destination tile; in each component one destination tile is named 24 times by the used slots of every tile.
All inputs are finite; a program needn't handle non-finite values. No bound on the sum of `sea_mask` on one device may be relied on, other than what follows from the above.
Results may differ from a plain program's by a relative error of at most 0.0015.
Values may be sent and summed in bfloat16 or wider, within the bound.
A program may use at most 192 MiB of HBM per device.

v0:
```python
import jax
import jax.numpy as jnp
from jax import lax
from jax.sharding import PartitionSpec as P

BLOCK_CELLS = 128
STEP_COUNT = 2


HIGHEST = lax.Precision.HIGHEST


def with_halo(block, sides, width):
    for axis, dim in sides:
        count = lax.axis_size(axis)
        forward = [(i, i + 1) for i in range(count - 1)]
        backward = [(target, source) for source, target in forward]
        low = lax.ppermute(
            lax.slice_in_dim(block, block.shape[dim] - width, None, axis=dim), axis, forward
        )
        high = lax.ppermute(lax.slice_in_dim(block, 0, width, axis=dim), axis, backward)
        block = jnp.concatenate([low, block, high], axis=dim)
    return block


def advance(extended, rates, mixing):
    center = extended[:, :, 1:-1, :]
    laplace = (
        extended[:, :, 2:, :]
        + extended[:, :, :-2, :]
        + jnp.roll(center, 1, axis=3)
        + jnp.roll(center, -1, axis=3)
        - 4.0 * center
    )
    vertical = jnp.einsum("flm,fmyx->flyx", mixing, center, precision=HIGHEST)
    return center + rates[:, None, None, None] * laplace + vertical


def local(
    model_state,
    sea_mask,
    diffusion,
    vertical_mix,
    export_mix,
    import_mix,
    pair_source,
    pair_tile,
    pair_block,
    pair_count,
    pair_weight,
):
    current = model_state[0]
    fields, levels, tile_rows, row_cells = current.shape
    channels = export_mix.shape[1]
    tile_count = lax.axis_size("tile")
    other_comp = 1 - lax.axis_index("comp")
    slot_count = pair_source.shape[1]
    block_count = tile_rows * row_cells // BLOCK_CELLS
    capacity = (2 * slot_count + tile_count - 1) // tile_count
    rates = diffusion[0]
    mixing = vertical_mix[0]
    exports = jnp.einsum("kf,fyx->kyx", export_mix[0], current[:, 0], precision=HIGHEST).astype(
        jnp.bfloat16
    )
    picked = exports.reshape(channels, block_count, BLOCK_CELLS)[:, pair_source[0]]
    contrib = jnp.einsum("kpb,pbc->pkc", picked, pair_weight[0], preferred_element_type=jnp.float32)
    contrib = contrib.astype(jnp.bfloat16).reshape(slot_count, channels * BLOCK_CELLS)
    is_live = jnp.arange(slot_count, dtype=jnp.int32) < pair_count[0, 0]
    targets = pair_tile[0]
    tile_hits = (targets[:, None] == jnp.arange(tile_count, dtype=jnp.int32)[None, :]) & is_live[
        :, None
    ]
    running = jnp.cumsum(tile_hits.astype(jnp.int32), axis=0)
    rank_in = jnp.sum(jnp.where(tile_hits, running, 0), axis=1) - 1
    slot_index = targets * capacity + rank_in
    placement = (
        jnp.arange(tile_count * capacity, dtype=jnp.int32)[:, None] == slot_index[None, :]
    ) & is_live[None, :]
    outbound = jnp.dot(
        placement.astype(jnp.bfloat16), contrib, preferred_element_type=jnp.float32
    ).astype(jnp.bfloat16)
    outbound = outbound.reshape(tile_count, capacity, channels * BLOCK_CELLS)
    out_blocks = jnp.sum(jnp.where(placement, pair_block[0][None, :] + 1, 0), axis=1) - 1
    out_blocks = out_blocks.reshape(tile_count, capacity)
    slab_ids = jnp.arange(2, dtype=jnp.int32)
    chosen = slab_ids == other_comp
    wide = jnp.where(chosen[:, None, None, None], outbound[None], jnp.zeros((), jnp.bfloat16))
    wide_index = jnp.where(chosen[:, None, None], out_blocks[None], -1)
    wide, wide_index = (wide, wide_index)
    received, received_index = (
        lax.all_to_all(
            wide.reshape(2 * tile_count, capacity, channels * BLOCK_CELLS),
            ("comp", "tile"),
            split_axis=0,
            concat_axis=0,
            tiled=True,
        ),
        lax.all_to_all(
            wide_index.reshape(2 * tile_count, capacity),
            ("comp", "tile"),
            split_axis=0,
            concat_axis=0,
            tiled=True,
        ),
    )
    for sweep in range(STEP_COUNT):
        extended = with_halo(current, (("tile", 2),), 1)
        current = advance(extended, rates, mixing)
    flattened = received.reshape(-1, channels * BLOCK_CELLS)
    flat_index = received_index.reshape(-1)
    owner_hits = (jnp.arange(block_count, dtype=jnp.int32)[:, None] == flat_index[None, :]).astype(
        jnp.bfloat16
    )
    gathered = jnp.dot(owner_hits, flattened, preferred_element_type=jnp.float32)
    forcing = jnp.einsum(
        "fk,nkb->fnb",
        import_mix[0],
        gathered.reshape(block_count, channels, BLOCK_CELLS),
        precision=HIGHEST,
    )
    forcing = forcing.reshape(fields, tile_rows, row_cells) * sea_mask[0].astype(jnp.float32)
    current = current.at[:, 0].add(forcing)
    return current[None]


def solution(mesh):
    return jax.shard_map(
        local,
        mesh=mesh,
        in_specs=(
            P("comp", None, None, "tile", None),
            P("comp", "tile", None),
            P("comp", None),
            P("comp", None, None, None),
            P("comp", None, None),
            P("comp", None, None),
            P("comp", "tile"),
            P("comp", "tile"),
            P("comp", "tile"),
            P("comp", "tile"),
            P("comp", "tile", None, None),
        ),
        out_specs=P("comp", None, None, "tile", None),
        check_vma=False,
    )
```

profile of v0, /device:TPU:11, one launch (start us, length us, event | category | flops | bytes accessed | tf_op | source)
XLA Modules:
  0.0 195.8 jit_solution(16412042111983854809)
XLA Ops:
  0.0 0.0 copy-start
  0.7 0.1 broadcast_in_dim.84
  0.8 0.1 broadcast_in_dim.85
  0.9 0.7 broadcast_add_fusion.1
  1.5 0.7 fusion.42
  2.2 0.6 reduce-window.6
  2.8 0.2 slice_reduce_fusion
  3.1 0.1 bitcast_bitcast_fusion
  3.1 0.7 fusion.40
  3.8 0.7 multiply_add_fusion
  4.5 0.2 select_reduce_fusion
  4.7 0.1 sub.27
  4.8 0.7 broadcast_select_fusion
  5.5 6.3 %all-to-all-start = ((s32[32,1,24]{2,1,0:T(1,128)}), s32[32,1,24]{2,1,0:T(1,128)S(1)}, u32[]{:S(2)}, u32[]{:S(2)}) async-start(s32[32,1,24]{2,1,0:T(1,128)} %broadcast_select_fusion), calls=%async_computation | async-start | bytes 32768 | tf_op jit(solution)/shard_map/all_to_all | solution.py:98
  11.8 0.7 compare_select_fusion
  12.5 6.5 %copy.93 = f32[1,4,12,32,1024]{4,2,3,1,0:T(8,128)S(1)} copy(f32[1,4,12,32,1024]{4,3,2,1,0:T(8,128)} %param.13) | data formatting | bytes 12582912 | tf_op args[0]
  19.0 0.0 copy-start.2
  19.0 3.2 %copy-done.2 = f32[1,4,12,32,1024]{4,2,3,1,0:T(8,128)} copy-done((f32[1,4,12,32,1024]{4,2,3,1,0:T(8,128)}, f32[1,4,12,32,1024]{4,2,3,1,0:T(8,128)S(1)}, u32[]{:S(2)}) %copy-start.2) | copy-done | bytes 6291480
  22.3 0.3 slice.133
  22.6 0.0 copy-done
  22.6 2.1 %convolution_convert_fusion.1 = bf16[16,32,1024]{2,0,1:T(8,128)(2,1)S(1)} fusion(f32[4,1,32,1024]{3,1,2,0:T(1,128)S(1)} %slice.133, f32[1,16,4]{1,2,0:T(4,128)S(1)} %copy-done), kind=kOutput, calls=%fused_computation.26 | convolution fusion | flops 25690112 | bytes 1573120 | tf_op jit(solution)/shard_map/kf,fyx->kyx/dot_general | solution.py:62
  24.7 0.6 copy.58
  25.3 0.5 reshape.183
  25.8 0.7 copy.59
  26.5 0.8 gather_fusion
  27.2 4.5 %fusion.18 = bf16[192,16,128]{2,1,0:T(8,128)(2,1)S(1)} fusion(bf16[1,192,128,128]{3,2,1,0:T(8,128)(2,1)} %param.23, bf16[192,16,128]{2,1,0:T(8,128)(2,1)S(1)} %gather_fusion), kind=kOutput, calls=%fused_computation.27 | convolution fusion | flops 101056512 | bytes 7864320 | tf_op jit(solution)/shard_map/kpb,pbc->pkc/dot_general | solution.py:66
  31.8 0.7 convolution_convert_fusion
  32.5 1.9 bitcast_select_fusion
  34.5 0.0 all-to-all-done
  34.5 5.9 %all-to-all-start.1 = ((bf16[32,24,2048]{2,1,0:T(8,128)(2,1)}), bf16[32,24,2048]{2,1,0:T(8,128)(2,1)}, u32[]{:S(2)}, u32[]{:S(2)}) async-start(bf16[32,24,2048]{2,1,0:T(8,128)(2,1)} %bitcast_select_fusion), calls=%async_computation.1 | async-start | bytes 6291456 | tf_op jit(solution)/shard_map/all_to_all | solution.py:91
  40.4 1.1 fusion.50
  41.4 2.3 %collective-permute-start = (f32[4,12,1,1024]{3,1,2,0:T(8,128)S(1)}, f32[4,12,1,1024]{3,1,2,0:T(8,128)S(1)}, u32[]{:S(2)}, u32[]{:S(2)}) collective-permute-start(f32[4,12,1,1024]{3,1,2,0:T(8,128)S(1)} %get-tuple-element.27), channel_id=1, source_target_pairs={{1,0},{2,1},{3,2},{4,3},{5,4},{6,5},{7,6},{8,7},{9,8},{10,9},{11,1... | collective-permute-start | bytes 589832 | tf_op jit(solution)/shard_map/ppermute | solution.py:21
  43.7 4.4 %collective-permute-start.1 = (f32[4,12,1,1024]{3,1,2,0:T(8,128)S(1)}, f32[4,12,1,1024]{3,1,2,0:T(8,128)S(1)}, u32[]{:S(2)}, u32[]{:S(2)}) collective-permute-start(f32[4,12,1,1024]{3,1,2,0:T(8,128)S(1)} %get-tuple-element.28), channel_id=1, source_target_pairs={{0,1},{1,2},{2,3},{3,4},{4,5},{5,6},{6,7},{7,8},{8,9},{9,10},{10,1... | collective-permute-start | bytes 589832 | tf_op jit(solution)/shard_map/ppermute | solution.py:18
  48.1 2.9 %fusion.49 = (f32[4,12,32,1]{3,1,2,0:T(8,128)S(1)}, f32[4,12,32,1]{3,1,2,0:T(8,128)}) fusion(f32[4,12,32,1024]{3,1,2,0:T(8,128)} %bitcast.78), kind=kLoop, calls=%fused_computation.74 | loop fusion | bytes 24576 | tf_op jit(solution)/shard_map/jit(_roll_static)/slice | solution.py:32
  51.0 13.0 %fusion.48 = (f32[4,12,32,1023]{3,1,2,0:T(8,128)}, f32[4,12,32,1023]{3,1,2,0:T(8,128)}) fusion(f32[4,12,32,1024]{3,1,2,0:T(8,128)} %bitcast.79), kind=kLoop, calls=%fused_computation.73 | loop fusion | bytes 25141248 | tf_op jit(solution)/shard_map/jit(_roll_static)/slice | solution.py:32
  64.0 0.0 copy-done.3
  64.0 0.6 broadcast.145
  64.6 0.7 reduce.7
  65.3 0.1 eq.80
  65.4 47.8 %collective-permute-done = f32[4,12,1,1024]{3,1,2,0:T(8,128)S(1)} collective-permute-done((f32[4,12,1,1024]{3,1,2,0:T(8,128)S(1)}, f32[4,12,1,1024]{3,1,2,0:T(8,128)S(1)}, u32[]{:S(2)}, u32[]{:S(2)}) %collective-permute-start) | collective-permute-done | bytes 196640 | tf_op jit(solution)/shard_map/ppermute | solution.py:21
  113.2 0.0 collective-permute-done.1
  113.2 0.7 copy-done.5
  113.9 0.0 copy-done.8
  113.9 19.6 %fusion.13 = f32[4,12,32,1024]{3,1,2,0:T(8,128)S(1)} fusion(f32[4,12,32,1024]{3,1,2,0:T(8,128)} %bitcast.80, f32[4,12,1,1024]{3,1,2,0:T(8,128)} %copy-done.5, f32[4,12,1,1024]{3,1,2,0:T(8,128)S(1)} %collective-permute-done, f32[4,12,32,1023]{3,1,2,0:T(8,128)} %get-tuple-element.24, f32[4,12,32,1]{3,1,2,0:T(8,128)} %get-tuple-element.26, ...), kind=kOutput, calls=%fused_computation.17 | convolution fusion | flops 245366784 | bytes 25561360 | tf_op jit(solution)/shard_map/flm,fmyx->flyx/dot_general | solution.py:35
  133.6 1.9 collective-permute-start.2
  135.5 0.0 copy-start.7
  135.5 4.5 %collective-permute-start.3 = (f32[4,12,1,1024]{3,1,2,0:T(8,128)S(1)}, f32[4,12,1,1024]{3,1,2,0:T(8,128)S(1)}, u32[]{:S(2)}, u32[]{:S(2)}) collective-permute-start(f32[4,12,1,1024]{3,1,2,0:T(8,128)S(1)} %get-tuple-element.22), channel_id=1, source_target_pairs={{0,1},{1,2},{2,3},{3,4},{4,5},{5,6},{6,7},{7,8},{8,9},{9,10},{10,1... | collective-permute-start | bytes 589832 | tf_op jit(solution)/shard_map/ppermute | solution.py:18
  140.1 7.4 %fusion.45 = (f32[4,12,32,1023]{3,1,2,0:T(8,128)}, f32[4,12,32,1023]{3,1,2,0:T(8,128)}) fusion(f32[4,12,32,1024]{3,1,2,0:T(8,128)S(1)} %fusion.13), kind=kLoop, calls=%fused_computation.70 | loop fusion | bytes 25141248 | tf_op jit(solution)/shard_map/jit(_roll_static)/slice | solution.py:32
  147.5 1.4 fusion.46
  148.8 0.0 collective-permute-done.2
  148.8 0.0 collective-permute-done.3
  148.9 0.7 copy-done.6
  149.6 0.0 copy-done.7
  149.6 15.8 %fusion.6 = f32[4,12,32,1024]{3,1,2,0:T(8,128)} fusion(f32[4,12,32,1024]{3,1,2,0:T(8,128)S(1)} %fusion.13, f32[4,12,1,1024]{3,1,2,0:T(8,128)} %copy-done.6, f32[4,12,1,1024]{3,1,2,0:T(8,128)S(1)} %collective-permute-done.2, f32[4,12,32,1023]{3,1,2,0:T(8,128)} %get-tuple-element.18, f32[4,12,32,1]{3,1,2,0:T(8,128)} %get-tuple-element.20, ...), kind=kOutput, calls=%fused_computation.8 | convolution fusion | flops 245366784 | bytes 25561360 | tf_op jit(solution)/shard_map/flm,fmyx->flyx/dot_general | solution.py:35
  165.3 0.0 all-to-all-done.1
  165.3 3.2 %copy.60 = bf16[2048,768]{1,0:T(8,128)(2,1)S(1)} copy(bf16[2048,768]{0,1:T(8,128)(2,1)} %bitcast.25) | data formatting | bytes 6291456 | tf_op jit(solution)/shard_map/dot_general | solution.py:114
  168.5 1.0 fusion.28
  169.6 0.0 copy-done.4
  169.6 2.4 %fusion.21 = f32[4,256,128]{2,0,1:T(4,128)S(1)} fusion(f32[256,16,128]{2,0,1:T(8,128)S(1)} %fusion.28, f32[1,4,16]{2,1,0:T(4,128)S(1)} %copy-done.4), kind=kOutput, calls=%fused_computation.28 | convolution fusion | flops 25165824 | bytes 2621696 | tf_op jit(solution)/shard_map/fk,nkb->fnb/dot_general | solution.py:115
  172.0 0.0 copy-start.1
  172.0 3.0 %fusion.30 = f32[1,4,1,32,1024]{4,2,3,1,0:T(1,128)S(1)} fusion(f32[4,12,32,1024]{3,1,2,0:T(8,128)} %fusion.6, f32[4,1,32,1024]{3,1,2,0:T(1,128)S(1)} %bitcast.85, f32[32,1024]{1,0:T(8,128)S(1)} %convert_bitcast_fusion), kind=kLoop, calls=%fused_computation.36 | loop fusion | flops 262144 | bytes 1703936 | tf_op jit(solution)/shard_map/broadcast_in_dim | solution.py:123
  175.1 11.0 %scatter-add.4 = f32[1,4,12,32,1024]{4,2,3,1,0:T(8,128)} dynamic-update-slice(f32[1,4,12,32,1024]{4,2,3,1,0:T(8,128)} %bitcast.82, f32[1,4,1,32,1024]{4,2,3,1,0:T(1,128)S(1)} %fusion.30, s32[]{:T(128)} %constant.54.clone.1, s32[]{:T(128)} %constant.54.clone.1, s32[]{:T(128)} %constant.54.clone.1, s32[]{:T(128)} %constant.54.clone.1, s32[]{:T(128)} %constant.54.clone.1) | dynamic-update-slice | bytes 1048580 | tf_op jit(solution)/shard_map/scatter-add | solution.py:122
  186.1 9.7 %copy.63 = f32[1,4,12,32,1024]{4,3,2,1,0:T(8,128)} copy(f32[1,4,12,32,1024]{4,2,3,1,0:T(8,128)} %scatter-add.4) | data formatting | bytes 12582912 | tf_op jit(solution)/shard_map/scatter-add | solution.py:122
  195.8 0.0 copy-done.1
  (17 shorter events, 0.2 us)
Async XLA Ops:
  0.0 22.6 %copy-start = (f32[1,16,4]{1,2,0:T(4,128)S(1)}, f32[1,16,4]{1,2,0:T(4,128)}, u32[]{:S(2)}) copy-start(f32[1,16,4]{1,2,0:T(4,128)} %param.17) | copy-start | bytes 772
  5.5 29.0 %all-to-all-start = ((s32[32,1,24]{2,1,0:T(1,128)}), s32[32,1,24]{2,1,0:T(1,128)S(1)}, u32[]{:S(2)}, u32[]{:S(2)}) async-start(s32[32,1,24]{2,1,0:T(1,128)} %broadcast_select_fusion), calls=%async_computation | async-start | bytes 32768 | tf_op jit(solution)/shard_map/all_to_all | solution.py:98
  19.0 3.2 %copy-start.2 = (f32[1,4,12,32,1024]{4,2,3,1,0:T(8,128)}, f32[1,4,12,32,1024]{4,2,3,1,0:T(8,128)S(1)}, u32[]{:S(2)}) copy-start(f32[1,4,12,32,1024]{4,2,3,1,0:T(8,128)S(1)} %copy.93) | copy-start | bytes 18874372
  34.5 130.9 %all-to-all-start.1 = ((bf16[32,24,2048]{2,1,0:T(8,128)(2,1)}), bf16[32,24,2048]{2,1,0:T(8,128)(2,1)}, u32[]{:S(2)}, u32[]{:S(2)}) async-start(bf16[32,24,2048]{2,1,0:T(8,128)(2,1)} %bitcast_select_fusion), calls=%async_computation.1 | async-start | bytes 6291456 | tf_op jit(solution)/shard_map/all_to_all | solution.py:91
  41.4 71.8 %collective-permute-start = (f32[4,12,1,1024]{3,1,2,0:T(8,128)S(1)}, f32[4,12,1,1024]{3,1,2,0:T(8,128)S(1)}, u32[]{:S(2)}, u32[]{:S(2)}) collective-permute-start(f32[4,12,1,1024]{3,1,2,0:T(8,128)S(1)} %get-tuple-element.27), channel_id=1, source_target_pairs={{1,0},{2,1},{3,2},{4,3},{5,4},{6,5},{7,6},{8,7},{9,8},{10,9},{11,1... | collective-permute-start | bytes 589832 | tf_op jit(solution)/shard_map/ppermute | solution.py:21
  43.7 69.5 %collective-permute-start.1 = (f32[4,12,1,1024]{3,1,2,0:T(8,128)S(1)}, f32[4,12,1,1024]{3,1,2,0:T(8,128)S(1)}, u32[]{:S(2)}, u32[]{:S(2)}) collective-permute-start(f32[4,12,1,1024]{3,1,2,0:T(8,128)S(1)} %get-tuple-element.28), channel_id=1, source_target_pairs={{0,1},{1,2},{2,3},{3,4},{4,5},{5,6},{6,7},{7,8},{8,9},{9,10},{10,1... | collective-permute-start | bytes 589832 | tf_op jit(solution)/shard_map/ppermute | solution.py:18
  51.0 13.0 %copy-start.3 = (s32[1,32,1024]{2,1,0:T(8,128)S(1)}, s32[1,32,1024]{2,1,0:T(8,128)}, u32[]{:S(2)}) copy-start(s32[1,32,1024]{2,1,0:T(8,128)} %param.14) | copy-start | bytes 393220
  51.0 62.9 %copy-start.8 = (f32[1,4]{1,0:T(1,128)S(1)}, f32[1,4]{1,0:T(1,128)}, u32[]{:S(2)}) copy-start(f32[1,4]{1,0:T(1,128)} %param.15) | copy-start | bytes 52
  113.2 0.7 copy-start.5
  133.6 15.2 %collective-permute-start.2 = (f32[4,12,1,1024]{3,1,2,0:T(8,128)S(1)}, f32[4,12,1,1024]{3,1,2,0:T(8,128)S(1)}, u32[]{:S(2)}, u32[]{:S(2)}) collective-permute-start(f32[4,12,1,1024]{3,1,2,0:T(8,128)S(1)} %get-tuple-element.21), channel_id=1, source_target_pairs={{1,0},{2,1},{3,2},{4,3},{5,4},{6,5},{7,6},{8,7},{9,8},{10,9},{11,1... | collective-permute-start | bytes 589832 | tf_op jit(solution)/shard_map/ppermute | solution.py:21
  135.5 14.0 %copy-start.7 = (f32[1,4,12,12]{3,1,2,0:T(4,128)S(1)}, f32[1,4,12,12]{3,1,2,0:T(4,128)}, u32[]{:S(2)}) copy-start(f32[1,4,12,12]{3,1,2,0:T(4,128)} %param.16) | copy-start | bytes 6916
  135.5 13.3 %collective-permute-start.3 = (f32[4,12,1,1024]{3,1,2,0:T(8,128)S(1)}, f32[4,12,1,1024]{3,1,2,0:T(8,128)S(1)}, u32[]{:S(2)}, u32[]{:S(2)}) collective-permute-start(f32[4,12,1,1024]{3,1,2,0:T(8,128)S(1)} %get-tuple-element.22), channel_id=1, source_target_pairs={{0,1},{1,2},{2,3},{3,4},{4,5},{5,6},{6,7},{7,8},{8,9},{9,10},{10,1... | collective-permute-start | bytes 589832 | tf_op jit(solution)/shard_map/ppermute | solution.py:18
  148.8 0.7 copy-start.6
  165.3 4.2 %copy-start.4 = (f32[1,4,16]{2,1,0:T(4,128)S(1)}, f32[1,4,16]{2,1,0:T(4,128)}, u32[]{:S(2)}) copy-start(f32[1,4,16]{2,1,0:T(4,128)} %param.18) | copy-start | bytes 772
  172.0 23.8 %copy-start.1 = (f32[1,16,4]{1,2,0:T(4,128)S(1)}, f32[1,16,4]{1,2,0:T(4,128)}, u32[]{:S(2)}) copy-start(f32[1,16,4]{1,2,0:T(4,128)} %param.17) | copy-start | bytes 772
where the time goes:
time: 197 us; the launch traced here: 196 us
  local copies, waits for them, and re-layouts  64.8 us (33%)
  waiting for transfers between devices  47.8 us (24%)
  matrix products  46.2 us (23%)
  starting transfers between devices  25.3 us (13%)
  other arithmetic  10.7 us (5%)
    ppermute x2, waiting for transfers between devices, with_halo(): lax.ppermute(lax.slice_in_dim(block, 0, width, axis=dim), axis, backward)  47.8 us
    dot_general x2, matrix products, advance(): vertical = jnp.einsum('flm,fmyx->flyx', mixing, center, precision=HIGHEST)  35.4 us
    slice x4, local copies, waits for them, and re-layouts, advance(): jnp.roll(center, -1, axis=3)  24.6 us
    scatter-add x2, local copies, waits for them, and re-layouts, local(): current = current.at[:, 0].add(forcing)  20.7 us
    unnamed x19, local copies, waits for them, and re-layouts  11.2 us
    ppermute x2, starting transfers between devices, with_halo(): lax.ppermute(lax.slice_in_dim(block, block.shape[dim] - width, None, axis...  8.91 us
    all_to_all x1, starting transfers between devices, local(): lax.all_to_all(wide_index.reshape(2 * tile_count, capacity), ('comp', 'ti...  6.33 us
    all_to_all x1, starting transfers between devices, local(): lax.all_to_all(wide.reshape(2 * tile_count, capacity, channels * BLOCK_CE...  5.88 us
  transfers between devices with their start and end apart: 6, of which 1 were waited for; matrix products, arithmetic and copies ran while one was open for 42% of the time, Pallas kernels for 0%

commit v1 on v0

v1 whole, which is shorter than its diff:
```python
import functools

import jax
import jax.numpy as jnp
from jax import lax
from jax.experimental import pallas as pl
from jax.experimental.pallas import tpu as pltpu
from jax.sharding import PartitionSpec as P

CELLS = 128
STEPS = 2
GROUP = 16
PAD = 8
LANE = 32
HIGHEST = lax.Precision.HIGHEST
MESH = pl.DeviceIdType.MESH
F32 = jnp.float32
BF16 = jnp.bfloat16


def iota(shape, dim):
    return lax.broadcasted_iota(jnp.int32, shape, dim)


def onehot(cond, dtype=F32):
    return jnp.where(cond, 1.0, 0.0).astype(dtype)


def exact_dot(a, b):
    return jnp.dot(a, b, precision=HIGHEST, preferred_element_type=F32)


def kron(mix_ref, f, fields, levels):
    mix = jnp.zeros((levels, levels), F32)
    for g in range(fields):
        mix = mix + jnp.where(f == g, 1.0, 0.0) * mix_ref[0, :, g, :]
    side = levels * GROUP
    left = onehot(iota((side, levels), 0) // GROUP == iota((side, levels), 1), BF16)
    right = onehot(iota((levels, side), 0) == iota((levels, side), 1) // GROUP, BF16)
    same = iota((side, side), 0) % GROUP == iota((side, side), 1) % GROUP
    high = mix.astype(BF16)
    low = (mix - high.astype(F32)).astype(BF16)

    def spread(part):
        part = jnp.dot(left, part, preferred_element_type=F32).astype(BF16)
        part = jnp.dot(part, right, preferred_element_type=F32)
        return jnp.where(same, part, 0.0).astype(BF16)

    return spread(high), spread(low)


def column(high, low, v, passes):
    levels, rows, width = v.shape
    vh = v.astype(BF16)
    vh2 = vh.reshape(levels * rows, width)
    out = jnp.dot(high, vh2, preferred_element_type=F32)
    out = out + jnp.dot(low, vh2, preferred_element_type=F32)
    if passes > 2:
        vl = (v - vh.astype(F32)).astype(BF16).reshape(levels * rows, width)
        out = out + jnp.dot(high, vl, preferred_element_type=F32)
    return out


def around(v):
    rows, width = v.shape
    return (
        pltpu.roll(v, 1, 0) + pltpu.roll(v, rows - 1, 0) + pltpu.roll(v, 1, 1) + pltpu.roll(v, width - 1, 1)
    )


def send_kernel(
    cap,
    chunk,
    lead,
    src_ref,
    count_ref,
    diff_ref,
    tile_ref,
    block_ref,
    state_ref,
    first_ref,
    last_ref,
    mix_ref,
    imix_ref,
    vmix_ref,
    w_ref,
    x_ref,
    recv_ref,
    ids_ref,
    out_ref,
    exports,
    contribs,
    mixed,
    payload,
    id_rows,
    im_send,
    im_recv,
    edges,
    halo,
    meta,
    ext,
    vert,
    pay_send_sem,
    pay_recv_sem,
    id_send_sem,
    id_recv_sem,
    small_send_sem,
    small_recv_sem,
):
    step = pl.program_id(0)
    me_c = lax.axis_index("comp")
    me_t = lax.axis_index("tile")
    n = recv_ref.shape[0]
    other = 1 - me_c
    above = lax.rem(me_t + 1, n)
    below = lax.rem(me_t + n - 1, n)
    fields, tile_rows, width = state_ref.shape[1], state_ref.shape[3], state_ref.shape[4]
    channels = mix_ref.shape[2]
    levels = x_ref.shape[2]
    xblocks = width // CELLS
    per_step = w_ref.shape[1]

    def halo_copies():
        return (
            pltpu.make_async_remote_copy(
                src_ref=edges.at[0],
                dst_ref=halo.at[1],
                send_sem=small_send_sem.at[0],
                recv_sem=small_recv_sem.at[0],
                device_id=(me_c, below),
                device_id_type=MESH,
            ),
            pltpu.make_async_remote_copy(
                src_ref=edges.at[1],
                dst_ref=halo.at[0],
                send_sem=small_send_sem.at[1],
                recv_sem=small_recv_sem.at[1],
                device_id=(me_c, above),
                device_id_type=MESH,
            ),
        )

    def mix_copy():
        return pltpu.make_async_remote_copy(
            src_ref=im_send,
            dst_ref=im_recv,
            send_sem=small_send_sem.at[2],
            recv_sem=small_recv_sem.at[2],
            device_id=(other, me_t),
            device_id_type=MESH,
        )

    def block_copies(to, source_slot):
        return (
            pltpu.make_async_remote_copy(
                src_ref=id_rows.at[to],
                dst_ref=ids_ref.at[source_slot],
                send_sem=id_send_sem.at[to],
                recv_sem=id_recv_sem.at[source_slot],
                device_id=(other, to),
                device_id_type=MESH,
            ),
            pltpu.make_async_remote_copy(
                src_ref=payload.at[to],
                dst_ref=recv_ref.at[source_slot],
                send_sem=pay_send_sem.at[to],
                recv_sem=pay_recv_sem.at[source_slot],
                device_id=(other, to),
                device_id_type=MESH,
            ),
        )

    @pl.when(step == 0)
    def _():
        barrier = pltpu.get_barrier_semaphore()

        def greet(t, carry):
            pl.semaphore_signal(barrier, inc=1, device_id=(other, t), device_id_type=MESH)
            return carry

        lax.fori_loop(0, n, greet, 0)
        pl.semaphore_signal(barrier, inc=1, device_id=(me_c, above), device_id_type=MESH)
        pl.semaphore_signal(barrier, inc=1, device_id=(me_c, below), device_id_type=MESH)
        im_send[...] = jnp.zeros_like(im_send)
        im_send[0:fields, 0:channels] = imix_ref[0]
        for f in range(fields):
            for r in range(2):
                edges[0, f, r] = first_ref[0, f, :, r, :].astype(BF16)
                edges[1, f, r] = last_ref[0, f, :, 6 + r, :].astype(BF16)
        pl.semaphore_wait(barrier, n + 2)
        for copy in halo_copies():
            copy.start()
        mix_copy().start()
        sub = 8
        rows = sub * channels
        cols = sub * fields
        left = onehot(iota((rows, channels), 0) % channels == iota((rows, channels), 1))
        right = onehot(iota((fields, cols), 0) == iota((fields, cols), 1) // sub)
        by_channel = lax.dot_general(
            left,
            mix_ref[0],
            (((1,), (1,)), ((), ())),
            precision=HIGHEST,
            preferred_element_type=F32,
        )
        spread = exact_dot(by_channel, right)
        spread = jnp.where(
            iota((rows, cols), 0) // channels == iota((rows, cols), 1) % sub, spread, 0.0
        )
        for g in range(tile_rows // sub):
            s = state_ref[0, :, 0, g * sub : (g + 1) * sub, :].reshape(cols, width)
            e = exact_dot(spread, s).astype(BF16)
            for y in range(sub):
                for xb in range(xblocks):
                    exports[(g * sub + y) * xblocks + xb] = e[
                        y * channels : (y + 1) * channels, xb * CELLS : (xb + 1) * CELLS
                    ]
        ext[...] = jnp.zeros_like(ext)

    @pl.when(step < lead)
    def _():
        for p in range(per_step):
            picked = exports[src_ref[0, step * per_step + p]]
            c = jnp.dot(picked, w_ref[0, p], preferred_element_type=F32)
            at = (p % GROUP) * channels
            contribs[step * (per_step // GROUP) + p // GROUP, at : at + channels, :] = c.astype(BF16)

    @pl.when(step == lead - 1)
    def _():
        mix_copy().wait()
        rows = fields * GROUP
        cols = GROUP * channels
        left = onehot(iota((rows, 8), 0) // GROUP == iota((rows, 8), 1))
        right = onehot(iota((CELLS, cols), 0) == iota((CELLS, cols), 1) % channels)
        blend = exact_dot(exact_dot(left, im_recv[...]), right)
        blend = jnp.where(iota((rows, cols), 0) % GROUP == iota((rows, cols), 1) // channels, blend, 0.0)
        high = blend.astype(BF16)
        low = (blend - high.astype(F32)).astype(BF16)
        slots = contribs.shape[0] * GROUP
        wide = mixed.shape[0]
        mixed[slots:, :] = jnp.zeros((wide - slots, fields * CELLS), BF16)
        for g in range(contribs.shape[0]):
            cb = contribs[g]
            m = jnp.dot(high, cb, preferred_element_type=F32) + jnp.dot(
                low, cb, preferred_element_type=F32
            )
            m = m.astype(BF16)
            for f in range(fields):
                mixed[g * GROUP : (g + 1) * GROUP, f * CELLS : (f + 1) * CELLS] = m[
                    f * GROUP : (f + 1) * GROUP, :
                ]
        meta[...] = jnp.zeros_like(meta)
        meta[0:1, 0:slots] = tile_ref[...]
        meta[1:2, 0:slots] = block_ref[...]
        lane = iota((1, wide), 1)
        live = lane < count_ref[0, 0]
        tiles = jnp.where(live, meta[0:1, :], -1)
        square_row = iota((wide, wide), 0)
        square_col = iota((wide, wide), 1)
        tile_square = jnp.broadcast_to(tiles, (wide, wide))
        tile_col = jnp.sum(
            jnp.where(square_row == square_col, tile_square, 0), axis=1, keepdims=True
        )
        same = (tile_col == tile_square) & (square_row < square_col)
        rank = jnp.sum(jnp.where(same, 1, 0), axis=0, keepdims=True)
        slot = jnp.where(live, tiles * chunk + rank, -1)
        dest = jnp.where(
            (iota((n, wide), 0) == tiles) & live,
            jnp.broadcast_to(meta[1:2, :] + 1, (n, wide)),
            0,
        )
        base = lax.rem(me_t, CELLS // LANE) * LANE
        spot = onehot(iota((CELLS, wide), 0) == rank + base, BF16)
        index_rows = lax.dot_general(
            dest.astype(F32).astype(BF16), spot, (((1,), (1,)), ((), ())), preferred_element_type=F32
        )
        for t in range(n):
            id_rows[t] = jnp.broadcast_to(index_rows[t : t + 1, :], (8, CELLS)).astype(BF16)
        for d in range(0, n, 8):
            place = onehot(iota((8 * chunk, wide), 0) + d * chunk == slot, BF16)
            block = jnp.dot(place, mixed[...], preferred_element_type=F32)
            for j in range(8):
                payload[d + j] = block[j * chunk : (j + 1) * chunk, :].astype(BF16)

        def send(k, carry):
            for copy in block_copies(lax.rem(me_t + k, n), me_t):
                copy.start()
            return carry

        lax.fori_loop(0, n, send, 0)
        for copy in halo_copies():
            copy.wait()

    @pl.when(step >= lead)
    def _():
        f = step - lead
        low_on = jnp.where(me_t > 0, 1.0, 0.0).astype(F32)
        high_on = jnp.where(me_t < n - 1, 1.0, 0.0).astype(F32)
        d = diff_ref[0, f]
        high, low = kron(vmix_ref, f, fields, levels)
        ext[:, PAD : PAD + tile_rows, :] = x_ref[0, 0]
        for r in range(2):
            ext[:, PAD - 2 + r : PAD - 1 + r, :] = (halo[0, f, r].astype(F32) * low_on)[:, None, :]
            at = PAD + tile_rows + r
            ext[:, at : at + 1, :] = (halo[1, f, r].astype(F32) * high_on)[:, None, :]
        total = tile_rows + 2 * PAD
        for g in range(total // GROUP):
            vert[g] = column(high, low, ext[:, g * GROUP : (g + 1) * GROUP, :], 3)
        row = iota((total, 1), 0)
        keep = jnp.where(row < PAD, low_on, jnp.where(row >= PAD + tile_rows, high_on, 1.0))
        for lev in range(levels):
            v = ext[lev]
            lift = vert[:, lev * GROUP : (lev + 1) * GROUP, :].reshape(total, width)
            out_ref[0, lev] = (v * (1.0 - 4.0 * d) + around(v) * d + lift) * keep

    @pl.when(step == pl.num_programs(0) - 1)
    def _():
        def finish(t, carry):
            for copy in block_copies(t, t):
                copy.wait()
            return carry

        lax.fori_loop(0, n, finish, 0)


def step_kernel(
    diff_ref,
    v_ref,
    vmix_ref,
    recv_ref,
    ids_ref,
    mask_ref,
    out_ref,
    vert,
    hits,
    packed,
):
    f = pl.program_id(0)
    n, chunk = recv_ref.shape[0], recv_ref.shape[1]
    levels, total, width = v_ref.shape[1], v_ref.shape[2], v_ref.shape[3]
    fields = vmix_ref.shape[2]
    rows = total - 2 * PAD
    xblocks = width // CELLS
    per_group = CELLS // LANE

    @pl.when(f == 0)
    def _():
        for g in range(n // per_group):
            ids = jnp.zeros((8, CELLS), F32)
            for j in range(per_group):
                ids = ids + ids_ref[g * per_group + j].astype(F32)
            ids = ids[0:1, :].astype(jnp.int32) - 1
            spot = jnp.where(ids >= 0, (ids % xblocks) * rows + ids // xblocks, -1)
            hits[:, g * CELLS : (g + 1) * CELLS] = onehot(
                iota((rows * xblocks, CELLS), 0) == spot, BF16
            )
        for t in range(n):
            packed[t, 0:chunk, :] = recv_ref[t]
            packed[t, chunk:, :] = jnp.zeros((LANE - chunk, packed.shape[2]), BF16)

    d = diff_ref[0, f]
    high, low = kron(vmix_ref, f, fields, levels)
    for g in range(rows // GROUP):
        at = PAD + g * GROUP
        vert[g] = column(high, low, v_ref[0, :, at : at + GROUP, :], 2)
    for lev in range(levels):
        v = v_ref[0, lev]
        lift = vert[:, lev * GROUP : (lev + 1) * GROUP, :].reshape(rows, width)
        near = v * (1.0 - 4.0 * d) + around(v) * d
        out_ref[0, 0, lev] = near[PAD : PAD + rows, :] + lift

    part = packed[:, :, pl.ds(pl.multiple_of(f * CELLS, CELLS), CELLS)].reshape(n * LANE, CELLS)
    forcing = jnp.dot(hits[...], part, preferred_element_type=F32)
    for xb in range(xblocks):
        cols = slice(xb * CELLS, (xb + 1) * CELLS)
        out_ref[0, 0, 0, :, cols] += forcing[xb * rows : (xb + 1) * rows, :] * mask_ref[
            0, :, cols
        ].astype(F32)


def local(
    model_state,
    sea_mask,
    diffusion,
    vertical_mix,
    export_mix,
    import_mix,
    pair_source,
    pair_tile,
    pair_block,
    pair_count,
    pair_weight,
):
    _, fields, levels, rows, width = model_state.shape
    channels = export_mix.shape[1]
    n = lax.axis_size("tile")
    slots = pair_source.shape[1]
    cap = (2 * slots + n - 1) // n
    chunk = -(-cap // 8) * 8
    wide = -(-slots // 128) * 128
    blocks = rows * width // CELLS
    total = rows + 2 * PAD
    lead = 4
    per_step = slots // lead
    last_rows = rows // 8 - 1

    vmix = vertical_mix.transpose(0, 2, 1, 3)
    smem = pl.BlockSpec(memory_space=pltpu.SMEM)
    hbm = pl.BlockSpec(memory_space=pl.ANY)

    def whole(shape):
        return pl.BlockSpec(shape, lambda i: (0,) * len(shape))

    def late(i):
        return lax.div(i, lead) * (i - lead)

    def early(i):
        return i + lax.div(i, lead) * (lead - 1 - i)

    received, ids, stepped = pl.pallas_call(
        functools.partial(send_kernel, cap, chunk, lead),
        grid=(lead + fields,),
        out_shape=(
            jax.ShapeDtypeStruct((n, chunk, fields * CELLS), BF16),
            jax.ShapeDtypeStruct((n, 8, CELLS), BF16),
            jax.ShapeDtypeStruct((fields, levels, total, width), F32),
        ),
        in_specs=[
            smem,
            smem,
            smem,
            whole((1, slots)),
            whole((1, slots)),
            whole((1, fields, 1, rows, width)),
            whole((1, fields, levels, 8, width)),
            pl.BlockSpec((1, fields, levels, 8, width), lambda i: (0, 0, 0, last_rows, 0)),
            whole((1, fields, channels)),
            whole((1, fields, channels)),
            whole((1, levels, fields, levels)),
            pl.BlockSpec((1, per_step, CELLS, CELLS), lambda i: (0, early(i), 0, 0)),
            pl.BlockSpec((1, 1, levels, rows, width), lambda i: (0, late(i), 0, 0, 0)),
        ],
        out_specs=(
            hbm,
            hbm,
            pl.BlockSpec((1, levels, total, width), lambda i: (late(i), 0, 0, 0)),
        ),
        scratch_shapes=[
            pltpu.VMEM((blocks, channels, CELLS), BF16),
            pltpu.VMEM((slots // GROUP, GROUP * channels, CELLS), BF16),
            pltpu.VMEM((wide, fields * CELLS), BF16),
            pltpu.VMEM((n, chunk, fields * CELLS), BF16),
            pltpu.VMEM((n, 8, CELLS), BF16),
            pltpu.VMEM((8, CELLS), F32),
            pltpu.VMEM((8, CELLS), F32),
            pltpu.VMEM((2, fields, 2, levels, width), BF16),
            pltpu.VMEM((2, fields, 2, levels, width), BF16),
            pltpu.VMEM((8, wide), jnp.int32),
            pltpu.VMEM((levels, total, width), F32),
            pltpu.VMEM((total // GROUP, levels * GROUP, width), F32),
            pltpu.SemaphoreType.DMA((n,)),
            pltpu.SemaphoreType.DMA((n,)),
            pltpu.SemaphoreType.DMA((n,)),
            pltpu.SemaphoreType.DMA((n,)),
            pltpu.SemaphoreType.DMA((3,)),
            pltpu.SemaphoreType.DMA((3,)),
        ],
        compiler_params=pltpu.CompilerParams(
            collective_id=0, has_side_effects=True, vmem_limit_bytes=58 << 20
        ),
    )(
        pair_source,
        pair_count,
        diffusion,
        pair_tile,
        pair_block,
        model_state,
        model_state,
        model_state,
        export_mix.transpose(0, 2, 1),
        import_mix,
        vmix,
        pair_weight,
        model_state,
    )

    return pl.pallas_call(
        step_kernel,
        grid=(fields,),
        out_shape=jax.ShapeDtypeStruct(model_state.shape, F32),
        in_specs=[
            smem,
            pl.BlockSpec((1, levels, total, width), lambda i: (i, 0, 0, 0)),
            whole((1, levels, fields, levels)),
            whole((n, chunk, fields * CELLS)),
            whole((n, 8, CELLS)),
            whole((1, rows, width)),
        ],
        out_specs=pl.BlockSpec((1, 1, levels, rows, width), lambda i: (0, i, 0, 0, 0)),
        scratch_shapes=[
            pltpu.VMEM((rows // GROUP, levels * GROUP, width), F32),
            pltpu.VMEM((blocks, n * LANE), BF16),
            pltpu.VMEM((n, LANE, fields * CELLS), BF16),
        ],
        compiler_params=pltpu.CompilerParams(vmem_limit_bytes=48 << 20),
    )(diffusion, stepped, vmix, received, ids, sea_mask)


def solution(mesh):
    return jax.shard_map(
        local,
        mesh=mesh,
        in_specs=(
            P("comp", None, None, "tile", None),
            P("comp", "tile", None),
            P("comp", None),
            P("comp", None, None, None),
            P("comp", None, None),
            P("comp", None, None),
            P("comp", "tile"),
            P("comp", "tile"),
            P("comp", "tile"),
            P("comp", "tile"),
            P("comp", "tile", None, None),
        ),
        out_specs=P("comp", None, None, "tile", None),
        check_vma=False,
    )
```

time: 197 us -> 41.7 us (0.21)
  the two profiles are of different devices: /device:TPU:11 before, /device:TPU:0 now
where the time goes in v1:
time: 41.7 us; the launch traced here: 41.4 us
  Pallas kernels  38.9 us (93%)
  local copies, waits for them, and re-layouts  1.76 us (4%)
  between operations  0.72 us (2%)
    pallas_call x1, Pallas kernels, local(): pl.pallas_call(functools.partial(send_kernel, cap, chunk, lead), grid=(le...  29.7 us
    pallas_call x1, Pallas kernels, local(): pl.pallas_call(step_kernel, grid=(fields,), out_shape=jax.ShapeDtypeStruc...  9.17 us
    unnamed x10, local copies, waits for them, and re-layouts  1.76 us

profile of v1, /device:TPU:0, one launch (start us, length us, event | category | flops | bytes accessed | tf_op | source)
XLA Modules:
  0.0 41.4 jit_solution(11118856080687161408)
XLA Ops:
  0.7 0.0 copy-start.1
  0.7 0.0 copy-start.2
  0.7 0.0 copy-start.4
  0.7 29.7 %shard_map.109 = (bf16[16,24,512]{2,1,0:T(8,128)(2,1)}, bf16[16,8,128]{2,1,0:T(8,128)(2,1)}, f32[4,12,48,1024]{3,2,1,0:T(8,128)}) custom-call(s32[1,192]{1,0:T(1,128)} %src_ref.1, s32[1,1]{1,0:T(1,128)S(6)} %copy.12.count_ref, f32[1,4]{1,0:T(1,128)} %diff_ref.3, s32[1,192]{1,0:T(1,128)} %tile_ref.1, s32[1,192]{1,0:T(1,128)} %block_ref.1, ...), custom_call_target="tpu_custom_call" | custom-call | tf_op jit(solution)/shard_map/pallas_call | solution.py:420
  30.4 0.0 copy-done.1
  30.4 0.0 copy-done.2
  30.4 0.0 copy-done.4
  30.4 0.0 copy-start
  30.4 1.0 %copy-done = bf16[16,24,512]{2,1,0:T(8,128)(2,1)S(1)} copy-done((bf16[16,24,512]{2,1,0:T(8,128)(2,1)S(1)}, bf16[16,24,512]{2,1,0:T(8,128)(2,1)}, u32[]{:S(2)}) %copy-start) | copy-done | bytes 393240
  31.4 0.0 copy-start.3
  31.4 0.8 %copy-done.3 = bf16[16,8,128]{2,1,0:T(8,128)(2,1)S(1)} copy-done((bf16[16,8,128]{2,1,0:T(8,128)(2,1)S(1)}, bf16[16,8,128]{2,1,0:T(8,128)(2,1)}, u32[]{:S(2)}) %copy-start.3) | copy-done | bytes 32792
  32.2 9.2 %shard_map.110 = f32[1,4,12,32,1024]{4,3,2,1,0:T(8,128)} custom-call(f32[1,4]{1,0:T(1,128)S(1)} %copy-done.4, f32[4,12,48,1024]{3,2,1,0:T(8,128)} %get-tuple-element.8.v_ref, f32[1,12,4,12]{3,2,1,0:T(4,128)S(1)} %bitcast.3, bf16[16,24,512]{2,1,0:T(8,128)(2,1)S(1)} %copy-done, bf16[16,8,128]{2,1,0:T(8,128)(2,1)S(1)} %copy-done.3, s32[1,32,1024]{2,1,0:T(8,128)S(1)} %copy-done.1), custom_call_target="tpu_custom_call" | custom-call | tf_op jit(solution)/shard_map/pallas_call | solution.py:487
Async XLA Ops:
  0.7 29.8 %copy-start.1 = (s32[1,32,1024]{2,1,0:T(8,128)S(1)}, s32[1,32,1024]{2,1,0:T(8,128)}, u32[]{:S(2)}) copy-start(s32[1,32,1024]{2,1,0:T(8,128)} %mask_ref.1) | copy-start | bytes 393220
  0.7 29.8 %copy-start.2 = (f32[1,4,12,12]{3,1,2,0:T(4,128)S(1)}, f32[1,4,12,12]{3,1,2,0:T(4,128)}, u32[]{:S(2)}) copy-start(f32[1,4,12,12]{3,1,2,0:T(4,128)} %param.14) | copy-start | bytes 6916
  0.7 29.8 %copy-start.4 = (f32[1,4]{1,0:T(1,128)S(1)}, f32[1,4]{1,0:T(1,128)}, u32[]{:S(2)}) copy-start(f32[1,4]{1,0:T(1,128)} %diff_ref.3) | copy-start | bytes 52
  30.4 1.0 %copy-start = (bf16[16,24,512]{2,1,0:T(8,128)(2,1)S(1)}, bf16[16,24,512]{2,1,0:T(8,128)(2,1)}, u32[]{:S(2)}) copy-start(bf16[16,24,512]{2,1,0:T(8,128)(2,1)} %get-tuple-element.9.recv_ref) | copy-start | bytes 1179652
  31.4 0.8 %copy-start.3 = (bf16[16,8,128]{2,1,0:T(8,128)(2,1)S(1)}, bf16[16,8,128]{2,1,0:T(8,128)(2,1)}, u32[]{:S(2)}) copy-start(bf16[16,8,128]{2,1,0:T(8,128)(2,1)} %get-tuple-element.10.ids_ref) | copy-start | bytes 98308

commit v2 on v1

--- a/solution.py
+++ b/solution.py
@@ -172,6 +172,14 @@
 
     @pl.when(step == 0)
     def _():
+        @pl.when(me_t == 0)
+        def _():
+            halo[0] = jnp.zeros(halo.shape[1:], BF16)
+
+        @pl.when(me_t == n - 1)
+        def _():
+            halo[1] = jnp.zeros(halo.shape[1:], BF16)
+
         barrier = pltpu.get_barrier_semaphore()
 
         def greet(t, carry):
@@ -188,8 +196,16 @@
                 edges[0, f, r] = first_ref[0, f, :, r, :].astype(BF16)
                 edges[1, f, r] = last_ref[0, f, :, 6 + r, :].astype(BF16)
         pl.semaphore_wait(barrier, n + 2)
-        for copy in halo_copies():
-            copy.start()
+        down, up = halo_copies()
+
+        @pl.when(me_t > 0)
+        def _():
+            down.start()
+
+        @pl.when(me_t < n - 1)
+        def _():
+            up.start()
+
         mix_copy().start()
         sub = 8
         rows = sub * channels
@@ -288,8 +304,17 @@
             return carry
 
         lax.fori_loop(0, n, send, 0)
-        for copy in halo_copies():
-            copy.wait()
+        down, up = halo_copies()
+
+        @pl.when(me_t > 0)
+        def _():
+            down.wait_send()
+            up.wait_recv()
+
+        @pl.when(me_t < n - 1)
+        def _():
+            up.wait_send()
+            down.wait_recv()
 
     @pl.when(step >= lead)
     def _():
@@ -502,7 +527,7 @@
             pltpu.VMEM((blocks, n * LANE), BF16),
             pltpu.VMEM((n, LANE, fields * CELLS), BF16),
         ],
-        compiler_params=pltpu.CompilerParams(vmem_limit_bytes=48 << 20),
+        compiler_params=pltpu.CompilerParams(vmem_limit_bytes=60 << 20),
     )(diffusion, stepped, vmix, received, ids, sea_mask)
 
 

time: 41.7 us -> 39.5 us (0.947)
  local copies, waits for them, and re-layouts: 1.76 us -> 0 us
    unnamed x10 -> x0, local copies, waits for them, and re-layouts: 1.76 us -> none
where the time goes in v2:
time: 39.5 us; the launch traced here: 39.3 us
  Pallas kernels  38.6 us (98%)
  between operations  0.66 us (2%)
    pallas_call x1, Pallas kernels, local(): pl.pallas_call(functools.partial(send_kernel, cap, chunk, lead), grid=(le...  29.3 us
    pallas_call x1, Pallas kernels, local(): pl.pallas_call(step_kernel, grid=(fields,), out_shape=jax.ShapeDtypeStruc...  9.32 us

profile of v2, /device:TPU:0, one launch (start us, length us, event | category | flops | bytes accessed | tf_op | source)
XLA Modules:
  0.0 39.3 jit_solution(15782684719159767957)
XLA Ops:
  0.7 29.3 %shard_map.109 = (bf16[16,24,512]{2,1,0:T(8,128)(2,1)}, bf16[16,8,128]{2,1,0:T(8,128)(2,1)}, f32[4,12,48,1024]{3,2,1,0:T(8,128)}) custom-call(s32[1,192]{1,0:T(1,128)} %src_ref.1, s32[1,1]{1,0:T(1,128)S(6)} %copy.12.count_ref, f32[1,4]{1,0:T(1,128)} %diff_ref.3, s32[1,192]{1,0:T(1,128)} %tile_ref.1, s32[1,192]{1,0:T(1,128)} %block_ref.1, ...), custom_call_target="tpu_custom_call" | custom-call | tf_op jit(solution)/shard_map/pallas_call | solution.py:445
  30.0 9.3 %shard_map.110 = f32[1,4,12,32,1024]{4,3,2,1,0:T(8,128)} custom-call(f32[1,4]{1,0:T(1,128)} %diff_ref.3, f32[4,12,48,1024]{3,2,1,0:T(8,128)} %get-tuple-element.8.v_ref, f32[1,12,4,12]{3,2,1,0:T(4,128)} %bitcast.3, bf16[16,24,512]{2,1,0:T(8,128)(2,1)} %get-tuple-element.9.recv_ref, bf16[16,8,128]{2,1,0:T(8,128)(2,1)} %get-tuple-element.10.ids_ref, ...), custom_call_target="tpu_custom_call" | custom-call | tf_op jit(solution)/shard_map/pallas_call | solution.py:512
